TPU v7x, 128 devices: a whole 4x4x4 slice. The times are simulated.
128 devices in a mesh: pts: 16 (over z, y), freq: 8 (over x, core).
Axes of the slice: x: 4, y: 4, z: 4, core: 2. Of those that a mesh axis runs over, the one named last changes fastest.
Arguments:
- spectra: bfloat16 [128, 5, 4096, 128], P('freq', None, 'pts'), parts along dimension 0, may hold values from -200 to 200, as said below
- weights: float32 [4096], P('pts'), as said below
Outputs:
- mode_shapes: bfloat16 [128, 5, 4096, 128], P('freq', None, 'pts'), parts along dimension 0
There are 8 independent parts, one for each index of `freq`. A program takes and returns all parts, laid end to end along the dimension named above; an argument that names none is the same for every part. Nothing has to cross between parts.
Inputs may be any that keep to these rules, and one draw needn't show every extreme that they name: `spectra`: each row (frequency, variable, point) and each block's column pair has its own scale; the complex columns are independent. `weights`: Positive; their sum is of order one.
All inputs are finite; a program needn't handle non-finite values.
Results may differ from a plain program's by a relative error of at most 0.0054.
Values sent between devices are 32-bit elements; how exact they have to be, the bound alone decides.
No kernel may reach another device: no remote copies, remote signals or barrier semaphores. Data moves between devices by JAX's collectives and lax.ppermute only.
A program may use at most 64 MiB of HBM per device.

v0:
```python
import jax
import jax.numpy as jnp
from jax import lax
from jax.sharding import PartitionSpec as P

NS_STEPS = 10


def split_parts(products):
    half_cols = products.shape[-1] // 2
    top_left = products[:, :half_cols, :half_cols]
    top_right = products[:, :half_cols, half_cols:]
    bottom_left = products[:, half_cols:, :half_cols]
    bottom_right = products[:, half_cols:, half_cols:]
    return (top_left + bottom_right, top_right - bottom_left)


def build_cross(real_part, imag_part):
    upper_row = jnp.concatenate([real_part, imag_part], 2)
    lower_row = jnp.concatenate([-imag_part, real_part], 2)
    return jnp.concatenate([upper_row, lower_row], 1)


def upper_of(cross_gram):
    order = cross_gram.shape[-1]
    places = jnp.arange(order)

    def eliminate(column, carry):
        working, factor = carry
        picker = (places == column).astype(jnp.float32)
        below = (places >= column).astype(jnp.float32)
        current = jnp.sum(working * picker[None, None, :], axis=2) * below[None, :]
        pivot = jnp.sqrt(jnp.sum(current * picker[None, :], axis=1))
        scaled = current / pivot[:, None]
        factor = factor + scaled[:, None, :] * picker[None, :, None]
        working = working - scaled[:, :, None] * scaled[:, None, :]
        return (working, factor)

    start = (cross_gram, jnp.zeros_like(cross_gram))
    working, factor = lax.fori_loop(0, order, eliminate, start)
    return factor


def solve_upper(upper_factor, right_side):
    order = upper_factor.shape[-1]
    places = jnp.arange(order)

    def back_step(count, solved):
        row = order - 1 - count
        picker = (places == row).astype(jnp.float32)
        factor_row = jnp.sum(upper_factor * picker[None, :, None], axis=1)
        side_row = jnp.sum(right_side * picker[None, :, None], axis=1)
        pivot = jnp.sum(factor_row * picker[None, :], axis=1)
        known = jnp.einsum("fj,fjk->fk", factor_row, solved, precision=lax.Precision.HIGHEST)
        value = (side_row - known) / pivot[:, None]
        return solved + picker[None, :, None] * value[:, None, :]

    return lax.fori_loop(0, order, back_step, jnp.zeros_like(right_side))


def gram_of(upper_factor):
    return jnp.einsum("fki,fkj->fij", upper_factor, upper_factor, precision=lax.Precision.HIGHEST)


def local(spectra, weights):
    freq_count, var_count, point_count, col_count = spectra.shape
    root_weights = jnp.sqrt(weights)
    weighted = (root_weights[None, None, :, None] * spectra.astype(jnp.float32)).astype(
        jnp.bfloat16
    )
    flat_rows = weighted.reshape(freq_count, var_count * point_count, col_count)
    products = jnp.einsum("frc,frd->fcd", flat_rows, flat_rows, preferred_element_type=jnp.float32)
    real_part, imag_part = split_parts(products)
    cross_gram = build_cross(real_part, imag_part)
    summed = lax.psum(cross_gram, "pts")
    upper_factor = upper_of(summed)
    frob_norm = jnp.sqrt(jnp.sum(upper_factor * upper_factor, axis=(1, 2)))
    polar = upper_factor / frob_norm[:, None, None]
    for sweep in range(NS_STEPS):
        inner_gram = gram_of(polar)
        polar = 1.5 * polar - 0.5 * jnp.einsum(
            "fij,fjk->fik", polar, inner_gram, precision=lax.Precision.HIGHEST
        )
    mapping = solve_upper(upper_factor, polar).astype(jnp.bfloat16)
    shapes = jnp.einsum("fvpc,fcd->fvpd", spectra, mapping, preferred_element_type=jnp.float32)
    return shapes.astype(jnp.bfloat16)


def solution(mesh):
    in_specs = (P("freq", None, "pts", None), P("pts"))
    out_specs = P("freq", None, "pts", None)
    return jax.shard_map(local, mesh=mesh, in_specs=in_specs, out_specs=out_specs, check_vma=False)
```

profile of v0, /device:TPU:0, one launch (start us, length us, event | category | flops | bytes accessed | tf_op | source)
XLA Modules:
  0.0 935.5 jit_solution(8490604428545319796)
XLA Ops:
  7.2 4.0 multiply_convert_fusion
  14.6 90.1 %all-reduce.2.cloned.1.call-done = f32[16,128,128]{2,1,0:T(8,128)} async-done(((f32[16,128,128]{2,1,0:T(8,128)}), f32[16,128,128]{2,1,0:T(8,128)}) %all-reduce.2.cloned.1.call-update) | async-done | bytes 1048592 | tf_op jit(solution)/shard_map/psum | solution.py:75
  104.7 568.0 %while.32 = (s32[]{:T(128)}, f32[16,128,128]{2,1,0:T(8,128)}, f32[16,128,128]{2,1,0:T(8,128)S(1)}, s32[]{:T(128)}, s32[]{:T(128)}) while((s32[]{:T(128)}, f32[16,128,128]{2,1,0:T(8,128)}, f32[16,128,128]{2,1,0:T(8,128)S(1)}, s32[]{:T(128)}, s32[]{:T(128)}) %tuple.73), condition=%wide.region_4.0_spmd.clone.clone, body=%wide.region_1.0_spmd.clone.clone.sunk | while | flops 1843699 | bytes 5287763 | solution.py:40
  106.5 2.7 select_add_fusion.2
  110.9 2.7 select_add_fusion.2
  115.3 2.7 select_add_fusion.2
  124.2 2.7 select_add_fusion.2
  133.1 2.7 select_add_fusion.2
  137.5 2.7 select_add_fusion.2
  141.9 2.7 select_add_fusion.2
  146.4 2.7 select_add_fusion.2
  150.8 2.7 select_add_fusion.2
  155.2 2.7 select_add_fusion.2
  159.7 2.7 select_add_fusion.2
  164.1 2.7 select_add_fusion.2
  168.5 2.7 select_add_fusion.2
  173.0 2.7 select_add_fusion.2
  177.4 2.7 select_add_fusion.2
  181.8 2.7 select_add_fusion.2
  186.3 2.7 select_add_fusion.2
  190.7 2.7 select_add_fusion.2
  195.1 2.7 select_add_fusion.2
  199.6 2.7 select_add_fusion.2
  208.4 2.7 select_add_fusion.2
  217.3 2.7 select_add_fusion.2
  221.7 2.7 select_add_fusion.2
  226.2 2.7 select_add_fusion.2
  230.6 2.7 select_add_fusion.2
  235.0 2.7 select_add_fusion.2
  705.7 208.5 %while.31 = (s32[]{:T(128)}, f32[16,128,128]{2,1,0:T(8,128)S(1)}, f32[16,128,128]{2,1,0:T(8,128)S(1)}, f32[16,128,128]{2,1,0:T(8,128)S(1)}, s32[]{:T(128)}, /*index=5*/s32[]{:T(128)}, s32[]{:T(128)}) while((s32[]{:T(128)}, f32[16,128,128]{2,1,0:T(8,128)S(1)}, f32[16,128,128]{2,1,0:T(8,128)S(1)}, f32[16,128,128]{2,1,0:T(8,128)S(1)}, ...), condition=%wide.region_10.0_spmd.clone, body=%wide.region_6.0_spmd.clone.sunk | while | flops 5247220 | bytes 5318896 | solution.py:58
  914.2 6.4 convert_bitcast_fusion
  920.6 7.8 copy.8
  (1540 shorter events, 737.8 us)
Async XLA Ops:
  6.5 98.1 %all-reduce.2.cloned.1.call-start = ((), (), s32[]{:S(2)}) async-start(), calls=%async_computation | async-start | bytes 2097152 | tf_op jit(solution)/shard_map/psum | solution.py:75
Sparse Core Ops, SparseCore 0:
  14.7 89.9 all-reduce.1
where the time goes:
time: 950 us; the launch traced here: 936 us
  other arithmetic  655 us (69%)
  matrix products  160 us (17%)
  waiting for transfers between devices  90.1 us (9%)
  between operations  13.8 us (1%)
  local copies, waits for them, and re-layouts  9.6 us (1%)
    add x128, other arithmetic, eliminate(): factor = factor + scaled[:, None, :] * picker[None, :, None]  340 us
    reduce_sum x128, other arithmetic, eliminate(): current = jnp.sum(working * picker[None, None, :], axis=2) * below[None, :]  200 us
    dot_general x128, matrix products, back_step(): jnp.einsum('fj,fjk->fk', factor_row, solved, precision=lax.Precision.HIGH...  120 us
    psum x1, waiting for transfers between devices, local(): summed = lax.psum(cross_gram, 'pts')  90.1 us
    reduce_sum x128, other arithmetic, back_step(): factor_row = jnp.sum(upper_factor * picker[None, :, None], axis=1)  33.5 us
    add x128, other arithmetic, back_step(): return solved + picker[None, :, None] * value[:, None, :]  25.6 us
    dot_general x10, matrix products, gram_of(): jnp.einsum('fki,fkj->fij', upper_factor, upper_factor, precision=lax.Prec...  19.4 us
  transfers between devices with their start and end apart: 1, of which 1 were waited for; matrix products, arithmetic and copies ran while one was open for 0% of the time, Pallas kernels for 0%

commit v1 on v0

--- a/solution.py
+++ b/solution.py
@@ -72,7 +72,9 @@
     products = jnp.einsum("frc,frd->fcd", flat_rows, flat_rows, preferred_element_type=jnp.float32)
     real_part, imag_part = split_parts(products)
     cross_gram = build_cross(real_part, imag_part)
-    summed = lax.psum(cross_gram, "pts")
+    summed = cross_gram
+    for hop in (1, 2, 4, 8):
+        summed = summed + lax.ppermute(summed, "pts", [(dev, dev ^ hop) for dev in range(16)])
     upper_factor = upper_of(summed)
     frob_norm = jnp.sqrt(jnp.sum(upper_factor * upper_factor, axis=(1, 2)))
     polar = upper_factor / frob_norm[:, None, None]

time: 950 us -> 530 us (0.56); the launches traced: 936 us -> 525 us
  other arithmetic: 655 us -> 244 us
  between operations: 13.8 us -> 0.44 us
  starting transfers between devices: 0.01 us -> 11.4 us
    add x128, other arithmetic: 340 us -> 84.3 us  [eliminate(): factor = factor + scaled[:, None, :] * picker[None, :, None]]
    reduce_sum x128, other arithmetic: 200 us -> 44 us  [eliminate(): current = jnp.sum(working * picker[None, None, :], axis=2) * below[None, :]]
    psum x1 -> x0, waiting for transfers between devices: 90.1 us -> none  [local(): summed = lax.psum(cross_gram, 'pts')]
    ppermute x0 -> x4, waiting for transfers between devices: none -> 88.5 us  [local(): lax.ppermute(summed, 'pts', [(dev, dev ^ hop) for dev in range(16)])]
    ppermute x0 -> x4, starting transfers between devices: none -> 11.4 us  [local(): lax.ppermute(summed, 'pts', [(dev, dev ^ hop) for dev in range(16)])]
  transfers between devices with their start and end apart: 1 -> 4, of which waited for: 1 -> 4; matrix products, arithmetic and copies ran while one was open for 0% -> 0% of each run, Pallas kernels for 0% -> 0%
where the time goes in v1:
time: 530 us; the launch traced here: 525 us
  other arithmetic  244 us (46%)
  matrix products  160 us (30%)
  waiting for transfers between devices  88.5 us (17%)
  starting transfers between devices  11.4 us (2%)
  loops' own time  10.6 us (2%)
  local copies, waits for them, and re-layouts  9.61 us (2%)
    dot_general x128, matrix products, back_step(): jnp.einsum('fj,fjk->fk', factor_row, solved, precision=lax.Precision.HIGH...  120 us
    ppermute x4, waiting for transfers between devices, local(): lax.ppermute(summed, 'pts', [(dev, dev ^ hop) for dev in range(16)])  88.5 us
    add x128, other arithmetic, eliminate(): factor = factor + scaled[:, None, :] * picker[None, :, None]  84.3 us
    reduce_sum x128, other arithmetic, eliminate(): current = jnp.sum(working * picker[None, None, :], axis=2) * below[None, :]  44 us
    reduce_sum x128, other arithmetic, back_step(): factor_row = jnp.sum(upper_factor * picker[None, :, None], axis=1)  33.5 us
    add x128, other arithmetic, back_step(): return solved + picker[None, :, None] * value[:, None, :]  25.4 us
    dot_general x10, matrix products, gram_of(): jnp.einsum('fki,fkj->fij', upper_factor, upper_factor, precision=lax.Prec...  19.4 us
    reduce_sum x128, other arithmetic, eliminate(): pivot = jnp.sqrt(jnp.sum(current * picker[None, :], axis=1))  14.6 us
  transfers between devices with their start and end apart: 4, of which 4 were waited for; matrix products, arithmetic and copies ran while one was open for 0% of the time, Pallas kernels for 0%

profile of v1, /device:TPU:0, one launch (start us, length us, event | category | flops | bytes accessed | tf_op | source)
XLA Modules:
  0.0 525.3 jit_solution(7766796865143851328)
XLA Ops:
  0.7 4.0 multiply_convert_fusion
  4.7 1.6 fusion.23
  7.1 1.8 collective-permute-start
  8.8 23.2 %collective-permute-done = f32[16,128,128]{2,1,0:T(8,128)S(1)} collective-permute-done((f32[16,128,128]{2,1,0:T(8,128)S(1)}, f32[16,128,128]{2,1,0:T(8,128)S(1)}, u32[]{:S(2)}, u32[]{:S(2)}) %collective-permute-start) | collective-permute-done | bytes 1048608 | tf_op jit(solution)/shard_map/ppermute | solution.py:77
  32.3 3.4 collective-permute-start.1
  35.8 22.3 %collective-permute-done.1 = f32[16,128,128]{2,1,0:T(8,128)S(1)} collective-permute-done((f32[16,128,128]{2,1,0:T(8,128)S(1)}, f32[16,128,128]{2,1,0:T(8,128)S(1)}, u32[]{:S(2)}, u32[]{:S(2)}) %collective-permute-start.1) | collective-permute-done | bytes 1048608 | tf_op jit(solution)/shard_map/ppermute | solution.py:77
  58.2 2.0 collective-permute-start.2
  60.3 21.4 %collective-permute-done.2 = f32[16,128,128]{2,1,0:T(8,128)S(1)} collective-permute-done((f32[16,128,128]{2,1,0:T(8,128)S(1)}, f32[16,128,128]{2,1,0:T(8,128)S(1)}, u32[]{:S(2)}, u32[]{:S(2)}) %collective-permute-start.2) | collective-permute-done | bytes 1048608 | tf_op jit(solution)/shard_map/ppermute | solution.py:77
  81.8 4.2 collective-permute-start.3
  86.0 21.6 %collective-permute-done.3 = f32[16,128,128]{2,1,0:T(8,128)} collective-permute-done((f32[16,128,128]{2,1,0:T(8,128)S(1)}, f32[16,128,128]{2,1,0:T(8,128)}, u32[]{:S(2)}, u32[]{:S(2)}) %collective-permute-start.3) | collective-permute-done | bytes 1048608 | tf_op jit(solution)/shard_map/ppermute | solution.py:77
  107.6 1.7 add.65
  109.2 160.3 %while.32 = (s32[]{:T(128)}, f32[16,128,128]{2,1,0:T(8,128)S(1)}, f32[16,128,128]{2,1,0:T(8,128)S(1)}, s32[]{:T(128)}, s32[]{:T(128)}) while((s32[]{:T(128)}, f32[16,128,128]{2,1,0:T(8,128)S(1)}, f32[16,128,128]{2,1,0:T(8,128)S(1)}, s32[]{:T(128)}, s32[]{:T(128)}) %tuple.73), condition=%wide.region_3.0_spmd.clone.clone, body=%wide.region_0.0_spmd.clone.clone.sunk | while | flops 1843699 | bytes 5287763 | solution.py:40
  269.7 1.9 fusion.21
  271.7 1.4 fusion.18
  273.1 1.9 fusion.24
  275.0 1.3 fusion.17
  276.3 1.9 fusion.25
  279.5 1.9 fusion.26
  281.5 1.5 fusion.15
  282.9 1.9 fusion.27
  284.9 1.3 fusion.14
  286.2 1.9 fusion.28
  288.1 1.3 fusion.13
  289.4 1.9 fusion.29
  291.3 1.3 fusion.12
  292.6 2.1 fusion.30
  294.8 1.3 fusion.11
  296.1 1.9 fusion.31
  299.3 1.9 fusion.32
  302.5 208.3 %while.31 = (s32[]{:T(128)}, f32[16,128,128]{2,1,0:T(8,128)S(1)}, f32[16,128,128]{2,1,0:T(8,128)S(1)}, f32[16,128,128]{2,1,0:T(8,128)S(1)}, s32[]{:T(128)}, /*index=5*/s32[]{:T(128)}, s32[]{:T(128)}) while((s32[]{:T(128)}, f32[16,128,128]{2,1,0:T(8,128)S(1)}, f32[16,128,128]{2,1,0:T(8,128)S(1)}, f32[16,128,128]{2,1,0:T(8,128)S(1)}, ...), condition=%wide.region_9.0_spmd.clone, body=%wide.region_5.0_spmd.clone.sunk | while | flops 5247220 | bytes 5318896 | solution.py:58
  510.9 6.4 %convert_bitcast_fusion = bf16[16,5,256,128]{2,3,1,0:T(8,128)(2,1)} fusion(bf16[16,5,256,128]{3,2,1,0:T(8,128)(2,1)} %param.6, f32[16,128,128]{2,1,0:T(8,128)S(1)} %get-tuple-element.182), kind=kOutput, calls=%fused_computation.21 | convolution fusion | flops 673972224 | bytes 11534336 | tf_op jit(solution)/shard_map/fvpc,fcd->fvpd/dot_general | solution.py:87
  517.2 7.8 %copy.8 = bf16[16,5,256,128]{3,2,1,0:T(8,128)(2,1)} copy(bf16[16,5,256,128]{2,3,1,0:T(8,128)(2,1)} %convert_bitcast_fusion) | data formatting | bytes 10485760 | tf_op jit(solution)/shard_map/convert_element_type | solution.py:88
  (1551 shorter events, 364.0 us)
Async XLA Ops:
  7.1 24.9 %collective-permute-start = (f32[16,128,128]{2,1,0:T(8,128)S(1)}, f32[16,128,128]{2,1,0:T(8,128)S(1)}, u32[]{:S(2)}, u32[]{:S(2)}) collective-permute-start(f32[16,128,128]{2,1,0:T(8,128)S(1)} %maximum_maximum_fusion), channel_id=1, source_target_pairs={{0,8},{8,0},{16,24},{24,16},{32,40},{40,32},{48,56},{56,48},{64,72... | collective-permute-start | bytes 3145736 | tf_op jit(solution)/shard_map/ppermute | solution.py:77
  32.3 25.7 %collective-permute-start.1 = (f32[16,128,128]{2,1,0:T(8,128)S(1)}, f32[16,128,128]{2,1,0:T(8,128)S(1)}, u32[]{:S(2)}, u32[]{:S(2)}) collective-permute-start(f32[16,128,128]{2,1,0:T(8,128)S(1)} %fusion.74), channel_id=1, source_target_pairs={{0,16},{8,24},{16,0},{24,8},{32,48},{40,56},{48,32},{56,40},{64,80... | collective-permute-start | bytes 3145736 | tf_op jit(solution)/shard_map/ppermute | solution.py:77
  58.2 23.5 %collective-permute-start.2 = (f32[16,128,128]{2,1,0:T(8,128)S(1)}, f32[16,128,128]{2,1,0:T(8,128)S(1)}, u32[]{:S(2)}, u32[]{:S(2)}) collective-permute-start(f32[16,128,128]{2,1,0:T(8,128)S(1)} %add.63), channel_id=1, source_target_pairs={{0,32},{8,40},{16,48},{24,56},{32,0},{40,8},{48,16},{56,24},{64,96... | collective-permute-start | bytes 3145736 | tf_op jit(solution)/shard_map/ppermute | solution.py:77
  81.8 4.2 copy-start
  81.8 25.7 %collective-permute-start.3 = (f32[16,128,128]{2,1,0:T(8,128)S(1)}, f32[16,128,128]{2,1,0:T(8,128)}, u32[]{:S(2)}, u32[]{:S(2)}) collective-permute-start(f32[16,128,128]{2,1,0:T(8,128)S(1)} %add.64), channel_id=1, source_target_pairs={{0,64},{8,72},{16,80},{24,88},{32,96},{40,104},{48,112},{56,120},{... | collective-permute-start | bytes 3145736 | tf_op jit(solution)/shard_map/ppermute | solution.py:77
